TPU v7x, 32 devices: a whole 2x2x4 slice. The times are simulated.
32 devices in a mesh: dp: 8 (over y, x, core), tensor: 4 (over z).
Axes of the slice: x: 2, y: 2, z: 4, core: 2. Of those that a mesh axis runs over, the one named last changes fastest.
Arguments:
- tokens: bfloat16 [4096, 3072], P('dp', 'tensor'), may hold values from -6 to 6
- cotangent: bfloat16 [4096, 1024], P('dp'), may hold values from -8 to 8
- weight: bfloat16 [3072, 1024], P('tensor'), may hold values from -6 to 6
- momentum: bfloat16 [8, 3072, 1024], P('dp', 'tensor'), may hold values from -1.1953125 to 1.1953125
- threshold: int32 [1024], replicated, may hold values from 2 to 8
Outputs:
- key_values: bfloat16 [4096, 1024], P(('dp', 'tensor'))
- input_grad: bfloat16 [4096, 3072], P('dp', 'tensor')
- new_momentum: bfloat16 [8, 3072, 1024], P('dp', 'tensor')
- new_weight: bfloat16 [3072, 1024], P('tensor', 'dp')
All inputs are finite; a program needn't handle non-finite values.
Results may differ from a plain program's by a relative error of at most 0.017.
Values may be sent and summed in bfloat16 or wider, within the bound.
No kernel may reach another device: no remote copies, remote signals or barrier semaphores. Data moves between devices by JAX's collectives and lax.ppermute only.
A program may use at most 64 MiB of HBM per device.

v0:
```python
import jax
import jax.numpy as jnp
from jax import lax
from jax.sharding import PartitionSpec as P

D = 3072


def per_device(tokens, cotangent, weight, momentum, threshold):
    inverse = D ** (-0.5)
    key_values = lax.psum_scatter(
        (jnp.dot(tokens, weight, preferred_element_type=jnp.float32) * inverse).astype(
            jnp.bfloat16
        ),
        "tensor",
        scatter_dimension=0,
        tiled=True,
    )
    input_grad = (
        lax.dot_general(
            cotangent, weight, (((1,), (1,)), ((), ())), preferred_element_type=jnp.float32
        )
        * inverse
    ).astype(jnp.bfloat16)
    gradient = (
        lax.dot_general(
            tokens, cotangent, (((0,), (0,)), ((), ())), preferred_element_type=jnp.float32
        )
        * inverse
    )
    fresh = (0.9 * momentum[0].astype(jnp.float32) + 0.1 * gradient).astype(jnp.bfloat16)
    column_share = weight.shape[1] // lax.axis_size("dp")
    arrived = lax.all_to_all(fresh[None], "dp", split_axis=2, concat_axis=0, tiled=True)
    votes = jnp.sum(jnp.clip(arrived.astype(jnp.float32) / 0.125, -1.0, 1.0), axis=0)
    first_column = lax.axis_index("dp") * column_share
    own_columns = lax.dynamic_slice_in_dim(weight, first_column, column_share, 1)
    own_limits = lax.dynamic_slice_in_dim(threshold, first_column, column_share, 0)
    update = jnp.clip(votes / own_limits.astype(jnp.float32)[None, :], -1.0, 1.0)
    new_weight = (own_columns.astype(jnp.float32) - 0.5 * update).astype(jnp.bfloat16)
    return (key_values, input_grad, fresh[None], new_weight)


def solution(mesh):
    in_specs = (P("dp", "tensor"), P("dp", None), P("tensor", None), P("dp", "tensor", None), P())
    out_specs = (
        P(("dp", "tensor"), None),
        P("dp", "tensor"),
        P("dp", "tensor", None),
        P("tensor", "dp"),
    )
    return jax.shard_map(
        per_device, mesh=mesh, in_specs=in_specs, out_specs=out_specs, check_vma=False
    )
```

profile of v0, /device:TPU:0, one launch (start us, length us, event | category | flops | bytes accessed | tf_op | source)
XLA Modules:
  0.0 78.0 jit_solution(1171594350504713559)
XLA Ops:
  7.2 0.0 copy-start
  7.2 3.2 %fusion.1 = bf16[1,768,1024]{2,1,0:T(8,128)(2,1)S(1)} fusion(bf16[512,768]{1,0:T(8,128)(2,1)} %param.5, bf16[512,1024]{1,0:T(8,128)(2,1)} %param.6, bf16[1,768,1024]{2,1,0:T(8,128)(2,1)} %param.8), kind=kOutput, calls=%fused_computation.5 | convolution fusion | flops 809238528 | bytes 4980736 | tf_op jit(solution)/shard_map/dot_general | solution.py:26
  10.3 0.0 copy-start.1
  10.4 5.9 %copy.11 = bf16[1,768,1024]{1,0,2:T(2,128)(2,1)} copy(bf16[1,768,1024]{2,1,0:T(8,128)(2,1)S(1)} %fusion.1) | data formatting | bytes 3145728 | tf_op jit(solution)/shard_map/broadcast_in_dim | solution.py:40
  16.3 0.0 copy-done.1
  16.3 0.5 broadcast.25
  16.8 11.2 %reduce.3 = bf16[1024,768]{1,0:T(8,128)(2,1)S(1)} reduce(bf16[1024,1,768]{2,1,0:T(2,128)(2,1)} %bitcast.18, bf16[]{:T(256)} %broadcast.25), dimensions={1}, to_apply=%bitcast.9.reduce_sub_computation | reduce | bytes 3145730
  28.0 1.9 %reshape.25 = bf16[8,2,49152]{2,1,0:T(2,128)(2,1)} reshape(bf16[1024,768]{1,0:T(8,128)(2,1)S(1)} %reduce.3) | data formatting | bytes 3145728
  29.9 5.2 %all-to-all-start = ((bf16[8,2,49152]{2,1,0:T(2,128)(2,1)}), bf16[8,2,49152]{2,1,0:T(2,128)(2,1)S(1)}, u32[]{:S(2)}, u32[]{:S(2)}) async-start(bf16[8,2,49152]{2,1,0:T(2,128)(2,1)} %reshape.25), calls=%async_computation.1 | async-start | bytes 3145728 | tf_op jit(solution)/shard_map/all_to_all | solution.py:33
  35.1 0.2 reduce-scatter.2.cloned.1.call-start
  35.3 0.0 copy-done
  35.3 3.1 %multiply_convert_fusion = bf16[512,1024]{1,0:T(8,128)(2,1)} fusion(bf16[512,768]{1,0:T(8,128)(2,1)} %param.5, bf16[768,1024]{1,0:T(8,128)(2,1)S(1)} %copy-done), kind=kOutput, calls=%fused_computation.3 | convolution fusion | flops 806354944 | bytes 3407872 | tf_op jit(solution)/shard_map/dot_general | solution.py:12
  38.4 0.0 reduce-scatter.2.cloned.1.call-update
  38.4 0.1 constant_dynamic-slice_fusion
  38.5 0.1 copy.14
  38.7 0.8 dynamic-slice_convert_fusion
  39.4 3.1 %multiply_convert_fusion.1 = bf16[512,768]{1,0:T(8,128)(2,1)} fusion(bf16[512,1024]{1,0:T(8,128)(2,1)} %param.6, bf16[768,1024]{1,0:T(8,128)(2,1)S(1)} %copy-done), kind=kOutput, calls=%fused_computation.4 | convolution fusion | flops 806092800 | bytes 3407872 | tf_op jit(solution)/shard_map/dot_general | solution.py:20
  42.5 13.5 %all-to-all-done = bf16[8,2,49152]{2,1,0:T(2,128)(2,1)S(1)} async-done(((bf16[8,2,49152]{2,1,0:T(2,128)(2,1)}), bf16[8,2,49152]{2,1,0:T(2,128)(2,1)S(1)}, u32[]{:S(2)}, u32[]{:S(2)}) %all-to-all-start) | async-done | bytes 1572896 | tf_op jit(solution)/shard_map/all_to_all | solution.py:33
  56.1 3.9 %reshape.26 = bf16[1024,1,768]{2,1,0:T(2,128)(2,1)} reshape(bf16[8,2,49152]{2,1,0:T(2,128)(2,1)S(1)} %all-to-all-done) | data formatting | bytes 3145728
  60.0 6.2 %multiply_clamp_fusion = f32[1,768,1024]{1,0,2:T(1,128)S(1)} fusion(bf16[1024,1,768]{2,1,0:T(2,128)(2,1)} %reshape.26), kind=kLoop, calls=%fused_computation.2 | loop fusion | flops 2359296 | bytes 4718592 | tf_op jit(solution)/shard_map/jit(clip)/min | solution.py:34
  66.2 1.9 %copy.13 = f32[1,768,1024]{1,2,0:T(8,128)} copy(f32[1,768,1024]{1,0,2:T(1,128)S(1)} %multiply_clamp_fusion) | data formatting | bytes 6291456
  68.1 2.1 %reduce.2 = f32[768,128]{0,1:T(8,128)S(1)} reduce(f32[768,8,128]{0,2,1:T(8,128)} %bitcast.19, f32[]{:T(128)} %constant.30.clone.1), dimensions={1}, to_apply=%region_1.2 | reduce | flops 688128 | bytes 3538948 | tf_op jit(solution)/shard_map/reduce_sum | solution.py:34
  70.2 0.1 subtract_convert_fusion
  70.4 0.8 %copy.12 = bf16[768,128]{1,0:T(8,128)(2,1)} copy(bf16[768,128]{0,1:T(8,128)(2,1)S(1)} %subtract_convert_fusion) | data formatting | bytes 393216
  (1 shorter events, 0.0 us)
Async XLA Ops:
  7.2 28.1 %copy-start = (bf16[768,1024]{1,0:T(8,128)(2,1)S(1)}, bf16[768,1024]{1,0:T(8,128)(2,1)}, u32[]{:S(2)}) copy-start(bf16[768,1024]{1,0:T(8,128)(2,1)} %param.7) | copy-start | bytes 4718596
  10.3 5.9 %copy-start.1 = (bf16[1,768,1024]{2,1,0:T(8,128)(2,1)}, bf16[1,768,1024]{2,1,0:T(8,128)(2,1)S(1)}, u32[]{:S(2)}) copy-start(bf16[1,768,1024]{2,1,0:T(8,128)(2,1)S(1)} %fusion.1) | copy-start | bytes 4718596
  29.9 26.2 %all-to-all-start = ((bf16[8,2,49152]{2,1,0:T(2,128)(2,1)}), bf16[8,2,49152]{2,1,0:T(2,128)(2,1)S(1)}, u32[]{:S(2)}, u32[]{:S(2)}) async-start(bf16[8,2,49152]{2,1,0:T(2,128)(2,1)} %reshape.25), calls=%async_computation.1 | async-start | bytes 3145728 | tf_op jit(solution)/shard_map/all_to_all | solution.py:33
  35.1 36.1 %reduce-scatter.2.cloned.1.call-start = ((), (), s32[]{:S(2)}) async-start(), calls=%async_computation.2 | async-start | bytes 1310720 | tf_op jit(solution)/shard_map/reduce_scatter | solution.py:11
Sparse Core Ops, SparseCore 0:
  38.7 28.9 reduce-scatter.1
where the time goes:
time: 78.4 us; the launch traced here: 78 us
  other arithmetic  20.5 us (26%)
  local copies, waits for them, and re-layouts  15.1 us (19%)
  between operations  14.1 us (18%)
  waiting for transfers between devices  13.5 us (17%)
  matrix products  9.39 us (12%)
  starting transfers between devices  5.41 us (7%)
    all_to_all x1, waiting for transfers between devices, per_device(): lax.all_to_all(fresh[None], 'dp', split_axis=2, concat_axis=0, tiled=True)  13.5 us
    unnamed x1, other arithmetic  11.2 us
    unnamed x10, local copies, waits for them, and re-layouts  9.15 us
    min x1, other arithmetic, per_device(): jnp.clip(arrived.astype(jnp.float32) / 0.125, -1.0, 1.0)  6.23 us
    broadcast_in_dim x1, local copies, waits for them, and re-layouts, per_device(): return (key_values, input_grad, fresh[None], new_weight)  5.9 us
    all_to_all x1, starting transfers between devices, per_device(): lax.all_to_all(fresh[None], 'dp', split_axis=2, concat_axis=0, tiled=True)  5.2 us
    dot_general x1, matrix products, per_device(): lax.dot_general(tokens, cotangent, (((0,), (0,)), ((), ())), preferred_el...  3.16 us
    dot_general x1, matrix products, per_device(): lax.dot_general(cotangent, weight, (((1,), (1,)), ((), ())), preferred_el...  3.13 us
  transfers between devices with their start and end apart: 2, of which 1 were waited for; matrix products, arithmetic and copies ran while one was open for 29% of the time, Pallas kernels for 0%

commit v1 on v0

--- a/solution.py
+++ b/solution.py
@@ -30,7 +30,10 @@
     )
     fresh = (0.9 * momentum[0].astype(jnp.float32) + 0.1 * gradient).astype(jnp.bfloat16)
     column_share = weight.shape[1] // lax.axis_size("dp")
-    arrived = lax.all_to_all(fresh[None], "dp", split_axis=2, concat_axis=0, tiled=True)
+    arrived = jnp.concatenate(
+        lax.all_to_all(jnp.stack(jnp.split(fresh[None], lax.axis_size("dp"), axis=2)), "dp", 0, 0),
+        axis=0,
+    )
     votes = jnp.sum(jnp.clip(arrived.astype(jnp.float32) / 0.125, -1.0, 1.0), axis=0)
     first_column = lax.axis_index("dp") * column_share
     own_columns = lax.dynamic_slice_in_dim(weight, first_column, column_share, 1)

time: 78.4 us -> 53.5 us (0.68)
  other arithmetic: 20.5 us -> 2.91 us
  local copies, waits for them, and re-layouts: 15.1 us -> 5.95 us
  waiting for transfers between devices: 13.5 us -> 16.9 us
  matrix products: 9.39 us -> 8.14 us
    unnamed x1 -> x0, other arithmetic: 11.2 us -> none
    min x1 -> x0, other arithmetic: 6.23 us -> none  [per_device(): jnp.clip(arrived.astype(jnp.float32) / 0.125, -1.0, 1.0)]
    broadcast_in_dim x1 -> x0, local copies, waits for them, and re-layouts: 5.9 us -> none  [per_device(): return (key_values, input_grad, fresh[None], new_weight)]
    unnamed x10 -> x15, local copies, waits for them, and re-layouts: 9.15 us -> 5.21 us
    all_to_all x1, waiting for transfers between devices: 13.5 us -> 16.9 us  [per_device(): lax.all_to_all(jnp.stack(jnp.split(fresh[None], lax.axis_size('dp'), axis...]
    dot_general x1, matrix products: 3.16 us -> 1.09 us  [per_device(): lax.dot_general(tokens, cotangent, (((0,), (0,)), ((), ())), preferred_el...]
    reduce_sum x1, other arithmetic: 2.1 us -> 0.45 us  [per_device(): jnp.sum(jnp.clip(arrived.astype(jnp.float32) / 0.125, -1.0, 1.0), axis=0)]
    convert_element_type x1, other arithmetic: 0.14 us -> 1.7 us  [per_device(): (own_columns.astype(jnp.float32) - 0.5 * update).astype(jnp.bfloat16)]
  transfers between devices with their start and end apart: 2 -> 2, of which waited for: 1 -> 1; matrix products, arithmetic and copies ran while one was open for 29% -> 25% of each run, Pallas kernels for 0% -> 0%
where the time goes in v1:
time: 53.5 us; the launch traced here: 53.3 us
  waiting for transfers between devices  16.9 us (32%)
  between operations  14.1 us (26%)
  matrix products  8.14 us (15%)
  local copies, waits for them, and re-layouts  5.95 us (11%)
  starting transfers between devices  5.23 us (10%)
  other arithmetic  2.91 us (5%)
    all_to_all x1, waiting for transfers between devices, per_device(): lax.all_to_all(jnp.stack(jnp.split(fresh[None], lax.axis_size('dp'), axis...  16.9 us
    unnamed x15, local copies, waits for them, and re-layouts  5.21 us
    all_to_all x1, starting transfers between devices, per_device(): lax.all_to_all(jnp.stack(jnp.split(fresh[None], lax.axis_size('dp'), axis...  5.2 us
    dot_general x1, matrix products, per_device(): jnp.dot(tokens, weight, preferred_element_type=jnp.float32) * inverse  3.75 us
    dot_general x1, matrix products, per_device(): lax.dot_general(cotangent, weight, (((1,), (1,)), ((), ())), preferred_el...  3.31 us
    convert_element_type x1, other arithmetic, per_device(): (own_columns.astype(jnp.float32) - 0.5 * update).astype(jnp.bfloat16)  1.7 us
    dot_general x1, matrix products, per_device(): lax.dot_general(tokens, cotangent, (((0,), (0,)), ((), ())), preferred_el...  1.09 us
  transfers between devices with their start and end apart: 2, of which 1 were waited for; matrix products, arithmetic and copies ran while one was open for 25% of the time, Pallas kernels for 0%

profile of v1, /device:TPU:0, one launch (start us, length us, event | category | flops | bytes accessed | tf_op | source)
XLA Modules:
  0.0 53.3 jit_solution(5248806894293349590)
XLA Ops:
  7.2 0.0 copy-start
  7.2 0.0 copy-start.3
  7.2 0.0 copy-start.2
  7.2 0.0 reduce-scatter.2.cloned.1.call-start
  7.2 3.7 %multiply_convert_fusion = bf16[512,1024]{1,0:T(8,128)(2,1)} fusion(bf16[512,768]{1,0:T(8,128)(2,1)} %param.5, bf16[768,1024]{1,0:T(8,128)(2,1)} %param.7), kind=kOutput, calls=%fused_computation.3 | convolution fusion | flops 806354944 | bytes 3407872 | tf_op jit(solution)/shard_map/dot_general | solution.py:12
  11.0 0.0 reduce-scatter.2.cloned.1.call-update
  11.0 0.0 copy-done
  11.0 0.0 copy-done.3
  11.0 1.1 %fusion.1 = bf16[1,768,1024]{2,1,0:T(8,128)(2,1)S(1)} fusion(bf16[512,768]{1,0:T(8,128)(2,1)S(1)} %copy-done.3, bf16[512,1024]{1,0:T(8,128)(2,1)S(1)} %copy-done, bf16[1,768,1024]{2,1,0:T(8,128)(2,1)S(1)} %copy-done.2), kind=kOutput, calls=%fused_computation.5 | convolution fusion | flops 809238528 | bytes 4980736 | tf_op jit(solution)/shard_map/dot_general | solution.py:26
  12.1 0.0 copy-start.1
  12.2 0.8 %fusion.9 = bf16[8,1,768,128]{3,2,1,0:T(8,128)(2,1)} fusion(bf16[1,768,1024]{2,1,0:T(8,128)(2,1)S(1)} %fusion.1), kind=kLoop, calls=%fused_computation.22 | loop fusion | bytes 393216
  13.0 0.7 %fusion.8 = bf16[8,1,768,128]{3,2,1,0:T(8,128)(2,1)} fusion(bf16[8,1,768,128]{3,2,1,0:T(8,128)(2,1)} %fusion.9, bf16[1,768,1024]{2,1,0:T(8,128)(2,1)S(1)} %fusion.1), kind=kLoop, calls=%fused_computation.20 | loop fusion | bytes 393216
  13.7 0.7 %fusion.7 = bf16[8,1,768,128]{3,2,1,0:T(8,128)(2,1)} fusion(bf16[8,1,768,128]{3,2,1,0:T(8,128)(2,1)} %fusion.8, bf16[1,768,1024]{2,1,0:T(8,128)(2,1)S(1)} %fusion.1), kind=kLoop, calls=%fused_computation.18 | loop fusion | bytes 393216
  14.4 0.7 %fusion.6 = bf16[8,1,768,128]{3,2,1,0:T(8,128)(2,1)} fusion(bf16[8,1,768,128]{3,2,1,0:T(8,128)(2,1)} %fusion.7, bf16[1,768,1024]{2,1,0:T(8,128)(2,1)S(1)} %fusion.1), kind=kLoop, calls=%fused_computation.16 | loop fusion | bytes 393216
  15.2 0.7 %fusion.5 = bf16[8,1,768,128]{3,2,1,0:T(8,128)(2,1)} fusion(bf16[8,1,768,128]{3,2,1,0:T(8,128)(2,1)} %fusion.6, bf16[1,768,1024]{2,1,0:T(8,128)(2,1)S(1)} %fusion.1), kind=kLoop, calls=%fused_computation.14 | loop fusion | bytes 393216
  15.9 0.7 %fusion.4 = bf16[8,1,768,128]{3,2,1,0:T(8,128)(2,1)} fusion(bf16[8,1,768,128]{3,2,1,0:T(8,128)(2,1)} %fusion.5, bf16[1,768,1024]{2,1,0:T(8,128)(2,1)S(1)} %fusion.1), kind=kLoop, calls=%fused_computation.12 | loop fusion | bytes 393216
  16.6 0.7 %fusion.3 = bf16[8,1,768,128]{3,2,1,0:T(8,128)(2,1)} fusion(bf16[8,1,768,128]{3,2,1,0:T(8,128)(2,1)} %fusion.4, bf16[1,768,1024]{2,1,0:T(8,128)(2,1)S(1)} %fusion.1), kind=kLoop, calls=%fused_computation.10 | loop fusion | bytes 393216
  17.3 0.7 %fusion.2 = bf16[8,1,768,128]{3,2,1,0:T(8,128)(2,1)} fusion(bf16[8,1,768,128]{3,2,1,0:T(8,128)(2,1)} %fusion.3, bf16[1,768,1024]{2,1,0:T(8,128)(2,1)S(1)} %fusion.1), kind=kLoop, calls=%fused_computation.8 | loop fusion | bytes 393216 | tf_op jit(solution)/shard_map/stack | solution.py:34
  18.1 5.2 %all-to-all-start = ((bf16[8,1,768,128]{3,2,1,0:T(8,128)(2,1)}), bf16[8,1,768,128]{3,2,1,0:T(8,128)(2,1)S(1)}, u32[]{:S(2)}, u32[]{:S(2)}) async-start(bf16[8,1,768,128]{3,2,1,0:T(8,128)(2,1)} %fusion.2), calls=%async_computation.1 | async-start | bytes 3145728 | tf_op jit(solution)/shard_map/all_to_all | solution.py:34
  23.3 0.8 %dynamic-slice_convert_fusion = f32[128]{0:T(128)S(1)} fusion(s32[1024]{0:T(1024)} %param.9, s32[]{:T(128)S(6)} %select_n.4), kind=kLoop, calls=%fused_computation.23 | loop fusion | flops 128 | bytes 1028 | tf_op jit(solution)/shard_map/convert_element_type | solution.py:41
  24.0 3.3 %multiply_convert_fusion.1 = bf16[512,768]{1,0:T(8,128)(2,1)} fusion(bf16[512,1024]{1,0:T(8,128)(2,1)S(1)} %copy-done, bf16[768,1024]{1,0:T(8,128)(2,1)} %param.7), kind=kOutput, calls=%fused_computation.4 | convolution fusion | flops 806092800 | bytes 3407872 | tf_op jit(solution)/shard_map/dot_general | solution.py:20
  27.4 16.9 %all-to-all-done = bf16[8,1,768,128]{3,2,1,0:T(8,128)(2,1)S(1)} async-done(((bf16[8,1,768,128]{3,2,1,0:T(8,128)(2,1)}), bf16[8,1,768,128]{3,2,1,0:T(8,128)(2,1)S(1)}, u32[]{:S(2)}, u32[]{:S(2)}) %all-to-all-start) | async-done | bytes 1572896 | tf_op jit(solution)/shard_map/all_to_all | solution.py:34
  44.3 0.5 clamp_reduce_fusion
  44.7 1.7 %subtract_convert_fusion = bf16[768,128]{1,0:T(8,128)(2,1)} fusion(f32[768,128]{1,0:T(8,128)S(1)} %clamp_reduce_fusion, f32[128]{0:T(128)S(1)} %dynamic-slice_convert_fusion, bf16[768,1024]{1,0:T(8,128)(2,1)} %param.7, s32[]{:T(128)S(6)} %select_n.4), kind=kLoop, calls=%fused_computation.6 | loop fusion | flops 589824 | bytes 786948 | tf_op jit(solution)/shard_map/convert_element_type | solution.py:42
  (3 shorter events, 0.0 us)
Async XLA Ops:
  7.2 3.9 %copy-start = (bf16[512,1024]{1,0:T(8,128)(2,1)S(1)}, bf16[512,1024]{1,0:T(8,128)(2,1)}, u32[]{:S(2)}) copy-start(bf16[512,1024]{1,0:T(8,128)(2,1)} %param.6) | copy-start | bytes 3145732
  7.2 3.9 %copy-start.3 = (bf16[512,768]{1,0:T(8,128)(2,1)S(1)}, bf16[512,768]{1,0:T(8,128)(2,1)}, u32[]{:S(2)}) copy-start(bf16[512,768]{1,0:T(8,128)(2,1)} %param.5) | copy-start | bytes 2359300
  7.2 3.9 %copy-start.2 = (bf16[1,768,1024]{2,1,0:T(8,128)(2,1)S(1)}, bf16[1,768,1024]{2,1,0:T(8,128)(2,1)}, u32[]{:S(2)}) copy-start(bf16[1,768,1024]{2,1,0:T(8,128)(2,1)} %param.8) | copy-start | bytes 4718596
  7.2 39.2 %reduce-scatter.2.cloned.1.call-start = ((), (), s32[]{:S(2)}) async-start(), calls=%async_computation.2 | async-start | bytes 1310720 | tf_op jit(solution)/shard_map/reduce_scatter | solution.py:11
  12.1 5.2 %copy-start.1 = (bf16[1,768,1024]{2,1,0:T(8,128)(2,1)}, bf16[1,768,1024]{2,1,0:T(8,128)(2,1)S(1)}, u32[]{:S(2)}) copy-start(bf16[1,768,1024]{2,1,0:T(8,128)(2,1)S(1)} %fusion.1) | copy-start | bytes 4718596
  18.1 26.2 %all-to-all-start = ((bf16[8,1,768,128]{3,2,1,0:T(8,128)(2,1)}), bf16[8,1,768,128]{3,2,1,0:T(8,128)(2,1)S(1)}, u32[]{:S(2)}, u32[]{:S(2)}) async-start(bf16[8,1,768,128]{3,2,1,0:T(8,128)(2,1)} %fusion.2), calls=%async_computation.1 | async-start | bytes 3145728 | tf_op jit(solution)/shard_map/all_to_all | solution.py:34
Sparse Core Ops, SparseCore 0:
  11.1 29.9 reduce-scatter.1
